TPU v7x, 32 devices: a whole 2x2x4 slice. The times are simulated.
32 devices in a mesh: col: 8 (over z, core), row: 4 (over y, x).
Axes of the slice: x: 2, y: 2, z: 4, core: 2. Of those that a mesh axis runs over, the one named last changes fastest.
Arguments:
- matrix: float32 [4096, 4096], P('row', 'col'), may hold values from -64 to 64, as said below
- plan: int32 [3, 8], replicated, may hold values from 0 to 1
Outputs:
- rotated: float32 [4096, 4096], P('row', 'col')
- coupling: float32 [3], replicated
Inputs may be any that keep to these rules, and one draw needn't show every extreme that they name: Entries of the matrix are real numbers; column scales differ between columns.
All inputs are finite; a program needn't handle non-finite values.
Results may differ from a plain program's by a relative error of at most 0.0003.
Values sent between devices are 32-bit elements; how exact they have to be, the bound alone decides.
A program may use at most 128 MiB of HBM per device.

v0:
```python
import jax
import jax.numpy as jnp
from jax import lax
from jax.sharding import PartitionSpec as P

SWEEPS = 2
STEPS = 3
highest = lax.Precision.HIGHEST
eps = 1e-06


def from_behind(x, axis, by):
    count = lax.axis_size(axis)
    return lax.ppermute(x, axis, [(i, (i + by) % count) for i in range(count)])


def product(first, second):
    return jnp.dot(first, second, precision=highest, preferred_element_type=jnp.float32)


def sweep_rotation(gram):
    width = gram.shape[0]
    eye = jnp.eye(width, dtype=jnp.float32)
    upper = jnp.triu(jnp.ones((width, width), jnp.float32), 1)
    rotation = eye
    for sweep in range(SWEEPS):
        diag = jnp.diagonal(gram)
        ratio = gram / (diag[:, None] + diag[None, :] + eps) * upper
        skew_raw = ratio - ratio.T
        scale = jnp.maximum(jnp.sqrt(jnp.sum(skew_raw * skew_raw)), 1.0)
        skew = skew_raw / scale
        square = product(skew, skew)
        system = eye - square
        inverse = 4.0 / 3.0 * eye - 4.0 / 9.0 * system
        for turn in range(2):
            inverse = product(inverse, 2.0 * eye - product(system, inverse))
        qmat = product(eye - 2.0 * skew + square, inverse)
        gram = product(qmat.T, product(gram, qmat))
        if sweep == 0:
            rotation = qmat
        else:
            rotation = product(rotation, qmat)
    return (rotation, gram)


def local_product(first, second):
    return lax.dot_general(
        first,
        second,
        (((0,), (0,)), ((), ())),
        precision=highest,
        preferred_element_type=jnp.float32,
    )


def pass_on(send):
    return from_behind(send, "col", 1)


def rotate_local(pair, gram, block):
    rotation, turned = sweep_rotation(gram)
    moved = product(pair, rotation)
    cross_sq = jnp.sum(turned[:block, block:] * turned[:block, block:])
    diag_sq = jnp.sum(jnp.diagonal(turned) ** 2)
    return (moved, turned, cross_sq, diag_sq)


def tally_step(cross_sq, diag_sq):
    return lax.psum((cross_sq, diag_sq), "col")


def finish_tally(tallies):
    crosses = jnp.stack([entry[0] for entry in tallies])
    diagonals = jnp.stack([entry[1] for entry in tallies])
    return jnp.log(crosses / diagonals)


def on_device(matrix, plan):
    block = matrix.shape[1] // 2
    position = lax.axis_index("col")
    pair_count = plan.shape[1]
    picker = jnp.arange(pair_count, dtype=jnp.int32) == position
    pair = matrix
    tallies = []
    gram = lax.psum(local_product(pair, pair), "row")
    for step in range(STEPS):
        moved, turned, cross_sq, diag_sq = rotate_local(pair, gram, block)
        tallies.append(tally_step(cross_sq, diag_sq))
        flag = jnp.sum(jnp.where(picker, plan[step], 0)) == 1
        left = moved[:, :block]
        right = moved[:, block:]
        send = jnp.where(flag, right, left)
        keep = jnp.where(flag, left, right)
        if step + 1 < STEPS:
            send_gram = jnp.where(flag, turned[block:, block:], turned[:block, :block])
            keep_gram = jnp.where(flag, turned[:block, :block], turned[block:, block:])
            received, received_gram = from_behind((send, send_gram), "col", 1)
            pair = jnp.concatenate([keep, received], axis=1)
            cross = lax.psum(local_product(keep, received), "row")
            top_rows = jnp.concatenate([keep_gram, cross], axis=1)
            low_rows = jnp.concatenate([cross.T, received_gram], axis=1)
            gram = jnp.concatenate([top_rows, low_rows], axis=0)
        else:
            received = pass_on(send)
            pair = jnp.concatenate([keep, received], axis=1)
    return (pair, finish_tally(tallies))


def solution(mesh):
    in_specs = (P("row", "col"), P())
    out_specs = (P("row", "col"), P())
    return jax.shard_map(
        on_device, mesh=mesh, in_specs=in_specs, out_specs=out_specs, check_vma=False
    )
```

profile of v0, /device:TPU:0, one launch (start us, length us, event | category | flops | bytes accessed | tf_op | source)
XLA Modules:
  0.0 446.2 jit_solution(14428658945225685061)
XLA Ops:
  8.8 4.5 %fusion.148 = f32[512,512]{1,0:T(8,128)} fusion(f32[1024,512]{1,0:T(8,128)S(1)} %copy-done), kind=kOutput, calls=%fused_computation.235 | convolution fusion | flops 3221225472 | bytes 3145728 | tf_op jit(solution)/shard_map/dot_general | solution.py:47
  19.0 49.7 %all-reduce.5.cloned.1.call-done = f32[512,512]{1,0:T(8,128)} async-done(((f32[512,512]{1,0:T(8,128)}), f32[512,512]{1,0:T(8,128)}) %all-reduce.5.cloned.1.call-update) | async-done | bytes 1048592 | tf_op jit(solution)/shard_map/psum | solution.py:85
  68.7 9.3 %gather_fusion = f32[512]{0:T(512)S(1)} fusion(f32[512,512]{1,0:T(8,128)} %all-reduce.5.cloned.1.call-done, s32[512]{0:T(512)S(1)} %bitcast.137), kind=kCustom, calls=%fused_computation | custom fusion | bytes 8192 | tf_op jit(solution)/shard_map/jit(diagonal)/cond/branch_0_fun/gather | solution.py:27
  90.2 4.2 fusion.141
  108.2 4.5 %gather_fusion.1 = f32[512]{0:T(512)S(1)} fusion(f32[512,512]{1,0:T(8,128)S(1)} %fusion.151, s32[512]{0:T(512)S(1)} %bitcast.138), kind=kCustom, calls=%fused_computation.1 | custom fusion | bytes 8192 | tf_op jit(solution)/shard_map/jit(diagonal)/cond/branch_0_fun/gather | solution.py:27
  118.3 5.2 %fusion.87 = f32[512,512]{1,0:T(8,128)S(1)} fusion(f32[512,512]{0,1:T(8,128)} %get-tuple-element.18, f32[]{:T(128)S(6)} %max.19), kind=kOutput, calls=%fused_computation.160 | convolution fusion | flops 1610874880 | bytes 2097156 | tf_op jit(solution)/shard_map/dot_general | solution.py:18
  130.0 3.6 fusion.35
  141.7 6.7 %convolution_bitcast_fusion = f32[1024,512]{0,1:T(8,128)S(1)} fusion(f32[512,512]{1,0:T(8,128)S(1)} %fusion.153, f32[1024,512]{1,0:T(8,128)S(1)} %copy-done), kind=kOutput, calls=%fused_computation.50 | convolution fusion | flops 3221225472 | bytes 5242880 | tf_op jit(solution)/shard_map/dot_general | solution.py:18
  152.6 12.2 %collective-permute-done = f32[1024,256]{0,1:T(8,128)S(1)} collective-permute-done((f32[1024,256]{0,1:T(8,128)S(1)}, f32[1024,256]{0,1:T(8,128)S(1)}, u32[]{:S(2)}, u32[]{:S(2)}) %collective-permute-start) | collective-permute-done | bytes 1048608 | tf_op jit(solution)/shard_map/ppermute | solution.py:14
  168.8 40.1 %all-reduce.7.cloned.1.call-done = f32[256,256]{0,1:T(8,128)} async-done(((f32[256,256]{0,1:T(8,128)}), f32[256,256]{0,1:T(8,128)}) %all-reduce.7.cloned.1.call-update) | async-done | bytes 262160 | tf_op jit(solution)/shard_map/psum | solution.py:99
  211.3 4.7 %gather_fusion.2 = f32[512]{0:T(512)S(1)} fusion(f32[512,512]{0,1:T(8,128)S(1)} %maximum_maximum_fusion, s32[512]{0:T(512)S(1)} %bitcast.139), kind=kCustom, calls=%fused_computation.2 | custom fusion | bytes 8192 | tf_op jit(solution)/shard_map/jit(diagonal)/cond/branch_0_fun/gather | solution.py:27
  239.5 4.5 %gather_fusion.3 = f32[512]{0:T(512)S(1)} fusion(f32[512,512]{1,0:T(8,128)S(1)} %fusion.158, s32[512]{0:T(512)S(1)} %bitcast.140), kind=kCustom, calls=%fused_computation.3 | custom fusion | bytes 8192 | tf_op jit(solution)/shard_map/jit(diagonal)/cond/branch_0_fun/gather | solution.py:27
  249.6 5.1 %fusion.88 = f32[512,512]{1,0:T(8,128)S(1)} fusion(f32[512,512]{0,1:T(8,128)} %get-tuple-element.16, f32[]{:T(128)S(6)} %max.21), kind=kOutput, calls=%fused_computation.161 | convolution fusion | flops 1610874880 | bytes 2097156 | tf_op jit(solution)/shard_map/dot_general | solution.py:18
  261.2 3.6 fusion.25
  280.4 12.2 %collective-permute-done.2 = f32[1024,256]{0,1:T(8,128)S(1)} collective-permute-done((f32[1024,256]{0,1:T(8,128)S(1)}, f32[1024,256]{0,1:T(8,128)S(1)}, u32[]{:S(2)}, u32[]{:S(2)}) %collective-permute-start.2) | collective-permute-done | bytes 1048608 | tf_op jit(solution)/shard_map/ppermute | solution.py:14
  297.5 4.5 %gather_fusion.6 = f32[512]{0:T(512)S(1)} fusion(f32[512,512]{0,1:T(8,128)S(1)} %copy-done.6, s32[512]{0:T(512)S(1)} %bitcast.141), kind=kCustom, calls=%fused_computation.6 | custom fusion | bytes 8192 | tf_op jit(solution)/shard_map/jit(diagonal)/cond/branch_0_fun/gather | solution.py:64
  302.7 4.5 %gather_fusion.7 = f32[512]{0:T(512)S(1)} fusion(f32[512,512]{0,1:T(8,128)S(1)} %fusion.162, s32[512]{0:T(512)S(1)} %bitcast.142), kind=kCustom, calls=%fused_computation.7 | custom fusion | bytes 8192 | tf_op jit(solution)/shard_map/jit(diagonal)/cond/branch_0_fun/gather | solution.py:64
  307.3 29.5 %all-reduce.9.cloned.1.call-done = f32[256,256]{0,1:T(8,128)} async-done(((f32[256,256]{0,1:T(8,128)}), f32[256,256]{0,1:T(8,128)}) %all-reduce.9.cloned.1.call-update) | async-done | bytes 262160 | tf_op jit(solution)/shard_map/psum | solution.py:99
  339.8 5.0 %gather_fusion.4 = f32[512]{0:T(512)S(1)} fusion(f32[512,512]{0,1:T(8,128)S(1)} %maximum_maximum_fusion.1, s32[512]{0:T(512)S(1)} %bitcast.143), kind=kCustom, calls=%fused_computation.4 | custom fusion | bytes 8192 | tf_op jit(solution)/shard_map/jit(diagonal)/cond/branch_0_fun/gather | solution.py:27
  362.9 4.5 %gather_fusion.5 = f32[512]{0:T(512)S(1)} fusion(f32[512,512]{1,0:T(8,128)S(1)} %fusion.165, s32[512]{0:T(512)S(1)} %bitcast.144), kind=kCustom, calls=%fused_computation.5 | custom fusion | bytes 8192 | tf_op jit(solution)/shard_map/jit(diagonal)/cond/branch_0_fun/gather | solution.py:27
  379.8 4.5 %fusion.89 = f32[512,512]{1,0:T(8,128)S(1)} fusion(f32[]{:T(128)S(6)} %max.23, f32[512,512]{1,0:T(8,128)} %copy.58, f32[512,512]{1,0:T(8,128)} %copy.57), kind=kOutput, calls=%fused_computation.162 | convolution fusion | flops 1611923456 | bytes 3145732 | tf_op jit(solution)/shard_map/dot_general | solution.py:18
  405.4 4.5 %gather_fusion.8 = f32[512]{0:T(512)S(1)} fusion(f32[512,512]{1,0:T(8,128)S(1)} %fusion.169, s32[512]{0:T(512)S(1)} %bitcast.145), kind=kCustom, calls=%fused_computation.8 | custom fusion | bytes 8192 | tf_op jit(solution)/shard_map/jit(diagonal)/cond/branch_0_fun/gather | solution.py:64
  411.3 17.8 %all-reduce = (f32[1]{0:T(128)}, f32[1]{0:T(128)}, f32[1]{0:T(128)}, f32[1]{0:T(128)}, f32[1]{0:T(128)}, /*index=5*/f32[1]{0:T(128)}) all-reduce(f32[1]{0:T(128)} %bitcast.18, f32[1]{0:T(128)} %bitcast.17, f32[1]{0:T(128)} %bitcast.16, f32[1]{0:T(128)} %bitcast.15, f32[1]{0:T(128)} %bitcast.14, ...), channel_id=1, replica_groups=mesh['col'=8,'row'=4] {'col'}, use_global_device_ids=true, to_apply=%region_23.24 | all-reduce | flops 6 | bytes 48 | tf_op jit(solution)/shard_map/psum | solution.py:69
  429.1 4.3 fusion.96
  (209 shorter events, 175.7 us)
Async XLA Ops:
  7.2 61.5 %all-reduce.5.cloned.1.call-start = ((), (), s32[]{:S(2)}) async-start(), calls=%async_computation | async-start | bytes 2097152 | tf_op jit(solution)/shard_map/psum | solution.py:85
  13.3 195.6 %all-reduce.7.cloned.1.call-start = ((), (), s32[]{:S(2)}) async-start(), calls=%async_computation.1 | async-start | bytes 524288 | tf_op jit(solution)/shard_map/psum | solution.py:99
  78.0 3.7 copy-start.2
  130.0 3.6 copy-start.12
  148.7 16.1 %copy-start.9 = (f32[1024,256]{0,1:T(8,128)}, f32[1024,256]{0,1:T(8,128)S(1)}, u32[]{:S(2)}) copy-start(f32[1024,256]{0,1:T(8,128)S(1)} %get-tuple-element.24) | copy-start | bytes 3145732
  148.7 16.1 %collective-permute-start = (f32[1024,256]{0,1:T(8,128)S(1)}, f32[1024,256]{0,1:T(8,128)S(1)}, u32[]{:S(2)}, u32[]{:S(2)}) collective-permute-start(f32[1024,256]{0,1:T(8,128)S(1)} %get-tuple-element.23), channel_id=1, source_target_pairs={{0,4},{4,8},{8,12},{12,16},{16,20},{20,24},{24,28},{28,0},{1,5},{5... | collective-permute-start | bytes 3145736 | tf_op jit(solution)/shard_map/ppermute | solution.py:14
  152.6 57.4 %copy-start.5 = (f32[512,512]{0,1:T(8,128)}, f32[512,512]{0,1:T(8,128)S(1)}, u32[]{:S(2)}) copy-start(f32[512,512]{0,1:T(8,128)S(1)} %fusion.155) | copy-start | bytes 3145732
  167.5 169.2 %all-reduce.9.cloned.1.call-start = ((), (), s32[]{:S(2)}) async-start(), calls=%async_computation.2 | async-start | bytes 524288 | tf_op jit(solution)/shard_map/psum | solution.py:99
  168.3 47.8 %copy-start.42 = (f32[256,256]{0,1:T(8,128)}, f32[256,256]{0,1:T(8,128)S(1)}, u32[]{:S(2)}) copy-start(f32[256,256]{0,1:T(8,128)S(1)} %get-tuple-element.26) | copy-start | bytes 786436
  168.3 41.8 %collective-permute-start.1 = (f32[256,256]{0,1:T(8,128)S(1)}, f32[256,256]{0,1:T(8,128)S(1)}, u32[]{:S(2)}, u32[]{:S(2)}) collective-permute-start(f32[256,256]{0,1:T(8,128)S(1)} %get-tuple-element.27), channel_id=1, source_target_pairs={{0,4},{4,8},{8,12},{12,16},{16,20},{20,24},{24,28},{28,0},{1,5},{5... | collective-permute-start | bytes 786440 | tf_op jit(solution)/shard_map/ppermute | solution.py:14
  210.0 6.0 %copy-start.36 = (f32[256,256]{0,1:T(8,128)}, f32[256,256]{0,1:T(8,128)S(1)}, u32[]{:S(2)}) copy-start(f32[256,256]{0,1:T(8,128)S(1)} %copy.43) | copy-start | bytes 786436
  210.1 6.0 %copy-start.47 = (f32[256,256]{0,1:T(8,128)}, f32[256,256]{0,1:T(8,128)S(1)}, u32[]{:S(2)}) copy-start(f32[256,256]{0,1:T(8,128)S(1)} %collective-permute-done.1) | copy-start | bytes 786436
  210.1 6.0 %copy-start.35 = (f32[256,256]{0,1:T(8,128)S(1)}, f32[256,256]{0,1:T(8,128)}, u32[]{:S(2)}) copy-start(f32[256,256]{0,1:T(8,128)} %all-reduce.7.cloned.1.call-done) | copy-start | bytes 786436
  216.7 5.1 %copy-start.15 = (f32[512,512]{1,0:T(8,128)}, f32[512,512]{1,0:T(8,128)S(1)}, u32[]{:S(2)}) copy-start(f32[512,512]{1,0:T(8,128)S(1)} %copy.44) | copy-start | bytes 3145732
  261.2 3.6 copy-start.14
  276.5 16.1 %collective-permute-start.2 = (f32[1024,256]{0,1:T(8,128)S(1)}, f32[1024,256]{0,1:T(8,128)S(1)}, u32[]{:S(2)}, u32[]{:S(2)}) collective-permute-start(f32[1024,256]{0,1:T(8,128)S(1)} %get-tuple-element.21), channel_id=1, source_target_pairs={{0,4},{4,8},{8,12},{12,16},{16,20},{20,24},{24,28},{28,0},{1,5},{5... | collective-permute-start | bytes 3145736 | tf_op jit(solution)/shard_map/ppermute | solution.py:14
  280.4 17.1 %copy-start.6 = (f32[512,512]{0,1:T(8,128)S(1)}, f32[512,512]{0,1:T(8,128)}, u32[]{:S(2)}) copy-start(f32[512,512]{0,1:T(8,128)} %copy-done.5) | copy-start | bytes 3145732
  296.9 41.0 %collective-permute-start.3 = (f32[256,256]{0,1:T(8,128)}, f32[256,256]{0,1:T(8,128)S(1)}, u32[]{:S(2)}, u32[]{:S(2)}) collective-permute-start(f32[256,256]{0,1:T(8,128)} %get-tuple-element.30), channel_id=1, source_target_pairs={{0,4},{4,8},{8,12},{12,16},{16,20},{20,24},{24,28},{28,0},{1,5},{5... | collective-permute-start | bytes 786440 | tf_op jit(solution)/shard_map/ppermute | solution.py:14
  302.1 36.6 %copy-start.40 = (f32[256,256]{0,1:T(8,128)S(1)}, f32[256,256]{0,1:T(8,128)}, u32[]{:S(2)}) copy-start(f32[256,256]{0,1:T(8,128)} %get-tuple-element.29) | copy-start | bytes 786436
  337.8 6.9 %copy-start.38 = (f32[256,256]{0,1:T(8,128)}, f32[256,256]{0,1:T(8,128)S(1)}, u32[]{:S(2)}) copy-start(f32[256,256]{0,1:T(8,128)S(1)} %copy.54) | copy-start | bytes 786436
  338.6 6.2 %copy-start.34 = (f32[256,256]{0,1:T(8,128)S(1)}, f32[256,256]{0,1:T(8,128)}, u32[]{:S(2)}) copy-start(f32[256,256]{0,1:T(8,128)} %all-reduce.9.cloned.1.call-done) | copy-start | bytes 786436
  338.6 6.2 %copy-start.45 = (f32[256,256]{0,1:T(8,128)S(1)}, f32[256,256]{0,1:T(8,128)}, u32[]{:S(2)}) copy-start(f32[256,256]{0,1:T(8,128)} %copy-done.44) | copy-start | bytes 786436
  401.0 32.4 %collective-permute-start.4 = (f32[1024,256]{0,1:T(8,128)}, f32[1024,256]{0,1:T(8,128)}, u32[]{:S(2)}, u32[]{:S(2)}) collective-permute-start(f32[1024,256]{0,1:T(8,128)} %get-tuple-element.20), channel_id=1, source_target_pairs={{0,4},{4,8},{8,12},{12,16},{16,20},{20,24},{24,28},{28,0},{1,5},{5... | collective-permute-start | bytes 3145736 | tf_op jit(solution)/shard_map/ppermute | solution.py:14
  433.4 6.0 %copy-start.1 = (f32[1024,512]{1,0:T(8,128)S(1)}, f32[1024,512]{1,0:T(8,128)}, u32[]{:S(2)}) copy-start(f32[1024,512]{1,0:T(8,128)} %param.2) | copy-start | bytes 6291460
  (34 other events, 64.9 us)
Sparse Core Ops, SparseCore 0:
  13.4 55.1 all-reduce.4
  167.7 41.2 all-reduce.6
  295.5 41.2 all-reduce.8
where the time goes:
time: 452 us; the launch traced here: 446 us
  waiting for transfers between devices  144 us (32%)
  matrix products  142 us (31%)
  local copies, waits for them, and re-layouts  82.9 us (18%)
  other arithmetic  38.6 us (9%)
  between operations  21.1 us (5%)
  blocking collectives  17.8 us (4%)
    dot_general x54, matrix products, product(): jnp.dot(first, second, precision=highest, preferred_element_type=jnp.floa...  134 us
    psum x2, waiting for transfers between devices, on_device(): cross = lax.psum(local_product(keep, received), 'row')  69.6 us
    psum x1, waiting for transfers between devices, on_device(): gram = lax.psum(local_product(pair, pair), 'row')  49.7 us
    gather x6, local copies, waits for them, and re-layouts, sweep_rotation(): diag = jnp.diagonal(gram)  32.6 us
    ppermute x5, waiting for transfers between devices, from_behind(): return lax.ppermute(x, axis, [(i, (i + by) % count) for i in range(count)])  24.4 us
    psum x1, blocking collectives, tally_step(): return lax.psum((cross_sq, diag_sq), 'col')  17.8 us
    reduce_sum x6, other arithmetic, sweep_rotation(): scale = jnp.maximum(jnp.sqrt(jnp.sum(skew_raw * skew_raw)), 1.0)  13.9 us
    gather x3, local copies, waits for them, and re-layouts, rotate_local(): diag_sq = jnp.sum(jnp.diagonal(turned) ** 2)  13.6 us
  transfers between devices with their start and end apart: 8, of which 5 were waited for; matrix products, arithmetic and copies ran while one was open for 9% of the time, Pallas kernels for 0%

commit v1 on v0

--- a/solution.py
+++ b/solution.py
@@ -96,7 +96,7 @@
             keep_gram = jnp.where(flag, turned[:block, :block], turned[block:, block:])
             received, received_gram = from_behind((send, send_gram), "col", 1)
             pair = jnp.concatenate([keep, received], axis=1)
-            cross = lax.psum(local_product(keep, received), "row")
+            cross = jnp.sum(lax.all_gather(local_product(keep, received), "row"), axis=0)
             top_rows = jnp.concatenate([keep_gram, cross], axis=1)
             low_rows = jnp.concatenate([cross.T, received_gram], axis=1)
             gram = jnp.concatenate([top_rows, low_rows], axis=0)

time: 452 us -> 413 us (0.914)
  waiting for transfers between devices: 144 us -> 111 us
  local copies, waits for them, and re-layouts: 82.9 us -> 77.5 us
    psum x2 -> x0, waiting for transfers between devices: 69.6 us -> none  [on_device(): cross = lax.psum(local_product(keep, received), 'row')]
    all_gather x0 -> x2, waiting for transfers between devices: none -> 29.3 us  [on_device(): lax.all_gather(local_product(keep, received), 'row')]
    ppermute x5, waiting for transfers between devices: 24.4 us -> 32 us  [from_behind(): return lax.ppermute(x, axis, [(i, (i + by) % count) for i in range(count)])]
    unnamed x101 -> x99, local copies, waits for them, and re-layouts: 9.29 us -> 8.52 us
  transfers between devices with their start and end apart: 8 -> 8, of which waited for: 5 -> 5; matrix products, arithmetic and copies ran while one was open for 9% -> 10% of each run, Pallas kernels for 0% -> 0%
where the time goes in v1:
time: 413 us; the launch traced here: 407 us
  matrix products  141 us (34%)
  waiting for transfers between devices  111 us (27%)
  local copies, waits for them, and re-layouts  77.5 us (19%)
  other arithmetic  38.1 us (9%)
  between operations  21.4 us (5%)
  blocking collectives  17.8 us (4%)
    dot_general x54, matrix products, product(): jnp.dot(first, second, precision=highest, preferred_element_type=jnp.floa...  133 us
    psum x1, waiting for transfers between devices, on_device(): gram = lax.psum(local_product(pair, pair), 'row')  49.6 us
    gather x6, local copies, waits for them, and re-layouts, sweep_rotation(): diag = jnp.diagonal(gram)  32.3 us
    ppermute x5, waiting for transfers between devices, from_behind(): return lax.ppermute(x, axis, [(i, (i + by) % count) for i in range(count)])  32 us
    all_gather x2, waiting for transfers between devices, on_device(): lax.all_gather(local_product(keep, received), 'row')  29.3 us
    psum x1, blocking collectives, tally_step(): return lax.psum((cross_sq, diag_sq), 'col')  17.8 us
    reduce_sum x6, other arithmetic, sweep_rotation(): scale = jnp.maximum(jnp.sqrt(jnp.sum(skew_raw * skew_raw)), 1.0)  13.8 us
    gather x3, local copies, waits for them, and re-layouts, rotate_local(): diag_sq = jnp.sum(jnp.diagonal(turned) ** 2)  13.6 us
  transfers between devices with their start and end apart: 8, of which 5 were waited for; matrix products, arithmetic and copies ran while one was open for 10% of the time, Pallas kernels for 0%

profile of v1, /device:TPU:0, one launch (start us, length us, event | category | flops | bytes accessed | tf_op | source)
XLA Modules:
  0.0 407.2 jit_solution(9720631350875730459)
XLA Ops:
  8.8 4.5 %fusion.148 = f32[512,512]{1,0:T(8,128)} fusion(f32[1024,512]{1,0:T(8,128)S(1)} %copy-done), kind=kOutput, calls=%fused_computation.235 | convolution fusion | flops 3221225472 | bytes 3145728 | tf_op jit(solution)/shard_map/dot_general | solution.py:47
  19.0 49.6 %all-reduce.3.cloned.1.call-done = f32[512,512]{1,0:T(8,128)} async-done(((f32[512,512]{1,0:T(8,128)}), f32[512,512]{1,0:T(8,128)}) %all-reduce.3.cloned.1.call-update) | async-done | bytes 1048592 | tf_op jit(solution)/shard_map/psum | solution.py:85
  68.7 9.1 %gather_fusion = f32[512]{0:T(512)S(1)} fusion(f32[512,512]{1,0:T(8,128)} %all-reduce.3.cloned.1.call-done, s32[512]{0:T(512)S(1)} %bitcast.139), kind=kCustom, calls=%fused_computation | custom fusion | bytes 8192 | tf_op jit(solution)/shard_map/jit(diagonal)/cond/branch_0_fun/gather | solution.py:27
  90.0 4.2 %fusion.141 = f32[512,512]{1,0:T(8,128)S(1)} fusion(f32[]{:T(128)S(6)} %max.18, f32[512,512]{1,0:T(8,128)} %divide_multiply_fusion, f32[512,512]{0,1:T(8,128)} %copy.59), kind=kOutput, calls=%fused_computation.230 | convolution fusion | flops 1611137024 | bytes 3145732 | tf_op jit(solution)/shard_map/dot_general | solution.py:18
  107.9 4.5 %gather_fusion.1 = f32[512]{0:T(512)S(1)} fusion(f32[512,512]{1,0:T(8,128)S(1)} %fusion.151, s32[512]{0:T(512)S(1)} %bitcast.140), kind=kCustom, calls=%fused_computation.1 | custom fusion | bytes 8192 | tf_op jit(solution)/shard_map/jit(diagonal)/cond/branch_0_fun/gather | solution.py:27
  118.1 5.2 %fusion.87 = f32[512,512]{1,0:T(8,128)S(1)} fusion(f32[512,512]{0,1:T(8,128)} %get-tuple-element.20, f32[]{:T(128)S(6)} %max.19), kind=kOutput, calls=%fused_computation.160 | convolution fusion | flops 1610874880 | bytes 2097156 | tf_op jit(solution)/shard_map/dot_general | solution.py:18
  129.7 3.6 fusion.35
  142.5 6.7 %convolution_bitcast_fusion = f32[1024,512]{0,1:T(8,128)S(1)} fusion(f32[512,512]{1,0:T(8,128)S(1)} %fusion.153, f32[1024,512]{1,0:T(8,128)S(1)} %copy-done), kind=kOutput, calls=%fused_computation.50 | convolution fusion | flops 3221225472 | bytes 5242880 | tf_op jit(solution)/shard_map/dot_general | solution.py:18
  149.5 16.0 %collective-permute-done = f32[1024,256]{0,1:T(8,128)S(1)} collective-permute-done((f32[1024,256]{0,1:T(8,128)S(1)}, f32[1024,256]{0,1:T(8,128)S(1)}, u32[]{:S(2)}, u32[]{:S(2)}) %collective-permute-start) | collective-permute-done | bytes 1048608 | tf_op jit(solution)/shard_map/ppermute | solution.py:14
  173.6 19.5 %all-gather.5.cloned.1.call-done = f32[1024,256]{1,0:T(8,128)} async-done(((f32[256,256]{1,0:T(8,128)}), f32[1024,256]{1,0:T(8,128)}) %all-gather.5.cloned.1.call-update) | async-done | bytes 1048592 | tf_op jit(solution)/shard_map/all_gather | solution.py:99
  194.7 4.7 %gather_fusion.2 = f32[512]{0:T(512)S(1)} fusion(f32[512,512]{0,1:T(8,128)S(1)} %maximum_maximum_fusion, s32[512]{0:T(512)S(1)} %bitcast.141), kind=kCustom, calls=%fused_computation.2 | custom fusion | bytes 8192 | tf_op jit(solution)/shard_map/jit(diagonal)/cond/branch_0_fun/gather | solution.py:27
  223.1 4.5 %gather_fusion.3 = f32[512]{0:T(512)S(1)} fusion(f32[512,512]{1,0:T(8,128)S(1)} %fusion.158, s32[512]{0:T(512)S(1)} %bitcast.142), kind=kCustom, calls=%fused_computation.3 | custom fusion | bytes 8192 | tf_op jit(solution)/shard_map/jit(diagonal)/cond/branch_0_fun/gather | solution.py:27
  233.0 5.1 %fusion.88 = f32[512,512]{1,0:T(8,128)S(1)} fusion(f32[512,512]{0,1:T(8,128)} %get-tuple-element.18, f32[]{:T(128)S(6)} %max.21), kind=kOutput, calls=%fused_computation.161 | convolution fusion | flops 1610874880 | bytes 2097156 | tf_op jit(solution)/shard_map/dot_general | solution.py:18
  242.4 3.6 fusion.25
  257.8 16.0 %collective-permute-done.2 = f32[1024,256]{0,1:T(8,128)S(1)} collective-permute-done((f32[1024,256]{0,1:T(8,128)S(1)}, f32[1024,256]{0,1:T(8,128)S(1)}, u32[]{:S(2)}, u32[]{:S(2)}) %collective-permute-start.2) | collective-permute-done | bytes 1048608 | tf_op jit(solution)/shard_map/ppermute | solution.py:14
  281.8 4.5 %gather_fusion.6 = f32[512]{0:T(512)S(1)} fusion(f32[512,512]{0,1:T(8,128)S(1)} %copy-done.9, s32[512]{0:T(512)S(1)} %bitcast.143), kind=kCustom, calls=%fused_computation.6 | custom fusion | bytes 8192 | tf_op jit(solution)/shard_map/jit(diagonal)/cond/branch_0_fun/gather | solution.py:64
  287.0 4.5 %gather_fusion.7 = f32[512]{0:T(512)S(1)} fusion(f32[512,512]{0,1:T(8,128)S(1)} %fusion.162, s32[512]{0:T(512)S(1)} %bitcast.144), kind=kCustom, calls=%fused_computation.7 | custom fusion | bytes 8192 | tf_op jit(solution)/shard_map/jit(diagonal)/cond/branch_0_fun/gather | solution.py:64
  291.6 9.9 %all-gather.7.cloned.1.call-done = f32[1024,256]{1,0:T(8,128)} async-done(((f32[256,256]{1,0:T(8,128)}), f32[1024,256]{1,0:T(8,128)}) %all-gather.7.cloned.1.call-update) | async-done | bytes 1048592 | tf_op jit(solution)/shard_map/all_gather | solution.py:99
  303.1 5.0 %gather_fusion.4 = f32[512]{0:T(512)S(1)} fusion(f32[512,512]{0,1:T(8,128)S(1)} %maximum_maximum_fusion.1, s32[512]{0:T(512)S(1)} %bitcast.145), kind=kCustom, calls=%fused_computation.4 | custom fusion | bytes 8192 | tf_op jit(solution)/shard_map/jit(diagonal)/cond/branch_0_fun/gather | solution.py:27
  326.1 4.5 %gather_fusion.5 = f32[512]{0:T(512)S(1)} fusion(f32[512,512]{1,0:T(8,128)S(1)} %fusion.165, s32[512]{0:T(512)S(1)} %bitcast.146), kind=kCustom, calls=%fused_computation.5 | custom fusion | bytes 8192 | tf_op jit(solution)/shard_map/jit(diagonal)/cond/branch_0_fun/gather | solution.py:27
  341.7 3.7 fusion.89
  366.5 4.5 %gather_fusion.8 = f32[512]{0:T(512)S(1)} fusion(f32[512,512]{1,0:T(8,128)S(1)} %fusion.169, s32[512]{0:T(512)S(1)} %bitcast.147), kind=kCustom, calls=%fused_computation.8 | custom fusion | bytes 8192 | tf_op jit(solution)/shard_map/jit(diagonal)/cond/branch_0_fun/gather | solution.py:64
  372.4 17.8 %all-reduce = (f32[1]{0:T(128)}, f32[1]{0:T(128)}, f32[1]{0:T(128)}, f32[1]{0:T(128)}, f32[1]{0:T(128)}, /*index=5*/f32[1]{0:T(128)}) all-reduce(f32[1]{0:T(128)} %bitcast.20, f32[1]{0:T(128)} %bitcast.19, f32[1]{0:T(128)} %bitcast.18, f32[1]{0:T(128)} %bitcast.17, f32[1]{0:T(128)} %bitcast.16, ...), channel_id=1, replica_groups=mesh['col'=8,'row'=4] {'col'}, use_global_device_ids=true, to_apply=%region_23.24 | all-reduce | flops 6 | bytes 48 | tf_op jit(solution)/shard_map/psum | solution.py:69
  390.2 4.2 %fusion.96 = f32[3]{0:T(128)} fusion(f32[1]{0:T(128)} %get-tuple-element.11, f32[1]{0:T(128)} %get-tuple-element.12, f32[1]{0:T(128)} %get-tuple-element.13, f32[1]{0:T(128)} %get-tuple-element.14, f32[1]{0:T(128)} %get-tuple-element.15, f32[1]{0:T(128)} %get-tuple-element.16), kind=kLoop, calls=%fused_computation.185 | loop fusion | flops 15 | bytes 36 | tf_op jit(solution)/shard_map/log | solution.py:75
  (209 shorter events, 170.3 us)
Async XLA Ops:
  7.2 61.5 %all-reduce.3.cloned.1.call-start = ((), (), s32[]{:S(2)}) async-start(), calls=%async_computation | async-start | bytes 2097152 | tf_op jit(solution)/shard_map/psum | solution.py:85
  13.3 179.8 %all-gather.5.cloned.1.call-start = ((), (), s32[]{:S(2)}) async-start(), calls=%async_computation.1 | async-start | bytes 1310720 | tf_op jit(solution)/shard_map/all_gather | solution.py:99
  77.7 3.7 copy-start.4
  129.7 3.6 copy-start.18
  149.4 18.9 %copy-start.15 = (f32[1024,256]{0,1:T(8,128)}, f32[1024,256]{0,1:T(8,128)S(1)}, u32[]{:S(2)}) copy-start(f32[1024,256]{0,1:T(8,128)S(1)} %get-tuple-element.26) | copy-start | bytes 3145732
  149.4 18.9 %copy-start.3 = (f32[512,512]{1,0:T(8,128)S(1)}, f32[512,512]{1,0:T(8,128)}, u32[]{:S(2)}) copy-start(f32[512,512]{1,0:T(8,128)} %copy-done.2) | copy-start | bytes 3145732
  149.4 16.1 %collective-permute-start = (f32[1024,256]{0,1:T(8,128)S(1)}, f32[1024,256]{0,1:T(8,128)S(1)}, u32[]{:S(2)}, u32[]{:S(2)}) collective-permute-start(f32[1024,256]{0,1:T(8,128)S(1)} %get-tuple-element.25), channel_id=1, source_target_pairs={{0,4},{4,8},{8,12},{12,16},{16,20},{20,24},{24,28},{28,0},{1,5},{5... | collective-permute-start | bytes 3145736 | tf_op jit(solution)/shard_map/ppermute | solution.py:14
  168.3 133.2 %all-gather.7.cloned.1.call-start = ((), (), s32[]{:S(2)}) async-start(), calls=%async_computation.2 | async-start | bytes 1310720 | tf_op jit(solution)/shard_map/all_gather | solution.py:99
  172.1 22.6 %copy-start.8 = (f32[512,512]{0,1:T(8,128)}, f32[512,512]{0,1:T(8,128)S(1)}, u32[]{:S(2)}) copy-start(f32[512,512]{0,1:T(8,128)S(1)} %fusion.155) | copy-start | bytes 3145732
  173.0 26.5 %copy-start.42 = (f32[256,256]{0,1:T(8,128)}, f32[256,256]{0,1:T(8,128)S(1)}, u32[]{:S(2)}) copy-start(f32[256,256]{0,1:T(8,128)S(1)} %get-tuple-element.28) | copy-start | bytes 786436
  173.0 21.6 %collective-permute-start.1 = (f32[256,256]{0,1:T(8,128)S(1)}, f32[256,256]{0,1:T(8,128)S(1)}, u32[]{:S(2)}, u32[]{:S(2)}) collective-permute-start(f32[256,256]{0,1:T(8,128)S(1)} %get-tuple-element.29), channel_id=1, source_target_pairs={{0,4},{4,8},{8,12},{12,16},{16,20},{20,24},{24,28},{28,0},{1,5},{5... | collective-permute-start | bytes 786440 | tf_op jit(solution)/shard_map/ppermute | solution.py:14
  194.6 4.9 %copy-start.36 = (f32[256,256]{0,1:T(8,128)}, f32[256,256]{0,1:T(8,128)S(1)}, u32[]{:S(2)}) copy-start(f32[256,256]{0,1:T(8,128)S(1)} %copy.66) | copy-start | bytes 786436
  194.6 4.9 %copy-start.46 = (f32[256,256]{0,1:T(8,128)}, f32[256,256]{0,1:T(8,128)S(1)}, u32[]{:S(2)}) copy-start(f32[256,256]{0,1:T(8,128)S(1)} %collective-permute-done.1) | copy-start | bytes 786436
  200.1 5.2 %copy-start.21 = (f32[512,512]{1,0:T(8,128)}, f32[512,512]{1,0:T(8,128)S(1)}, u32[]{:S(2)}) copy-start(f32[512,512]{1,0:T(8,128)S(1)} %copy.67) | copy-start | bytes 3145732
  223.1 5.9 %copy-start.12 = (f32[512,512]{0,1:T(8,128)S(1)}, f32[512,512]{0,1:T(8,128)}, u32[]{:S(2)}) copy-start(f32[512,512]{0,1:T(8,128)} %copy.62) | copy-start | bytes 3145732
  242.4 3.6 copy-start.20
  257.8 16.1 %copy-start.13 = (f32[1024,256]{0,1:T(8,128)}, f32[1024,256]{0,1:T(8,128)S(1)}, u32[]{:S(2)}) copy-start(f32[1024,256]{0,1:T(8,128)S(1)} %get-tuple-element.24) | copy-start | bytes 3145732
  257.8 16.1 %collective-permute-start.2 = (f32[1024,256]{0,1:T(8,128)S(1)}, f32[1024,256]{0,1:T(8,128)S(1)}, u32[]{:S(2)}, u32[]{:S(2)}) collective-permute-start(f32[1024,256]{0,1:T(8,128)S(1)} %get-tuple-element.23), channel_id=1, source_target_pairs={{0,4},{4,8},{8,12},{12,16},{16,20},{20,24},{24,28},{28,0},{1,5},{5... | collective-permute-start | bytes 3145736 | tf_op jit(solution)/shard_map/ppermute | solution.py:14
  281.2 26.9 %copy-start.40 = (f32[256,256]{0,1:T(8,128)}, f32[256,256]{0,1:T(8,128)S(1)}, u32[]{:S(2)}) copy-start(f32[256,256]{0,1:T(8,128)S(1)} %get-tuple-element.31) | copy-start | bytes 786436
  281.2 21.8 %collective-permute-start.3 = (f32[256,256]{0,1:T(8,128)S(1)}, f32[256,256]{0,1:T(8,128)S(1)}, u32[]{:S(2)}, u32[]{:S(2)}) collective-permute-start(f32[256,256]{0,1:T(8,128)S(1)} %get-tuple-element.32), channel_id=1, source_target_pairs={{0,4},{4,8},{8,12},{12,16},{16,20},{20,24},{24,28},{28,0},{1,5},{5... | collective-permute-start | bytes 786440 | tf_op jit(solution)/shard_map/ppermute | solution.py:14
  302.9 5.2 %copy-start.38 = (f32[256,256]{0,1:T(8,128)}, f32[256,256]{0,1:T(8,128)S(1)}, u32[]{:S(2)}) copy-start(f32[256,256]{0,1:T(8,128)S(1)} %copy.76) | copy-start | bytes 786436
  302.9 5.1 %copy-start.44 = (f32[256,256]{0,1:T(8,128)}, f32[256,256]{0,1:T(8,128)S(1)}, u32[]{:S(2)}) copy-start(f32[256,256]{0,1:T(8,128)S(1)} %collective-permute-done.3) | copy-start | bytes 786436
  362.1 32.4 %collective-permute-start.4 = (f32[1024,256]{0,1:T(8,128)}, f32[1024,256]{0,1:T(8,128)}, u32[]{:S(2)}, u32[]{:S(2)}) collective-permute-start(f32[1024,256]{0,1:T(8,128)} %get-tuple-element.22), channel_id=1, source_target_pairs={{0,4},{4,8},{8,12},{12,16},{16,20},{20,24},{24,28},{28,0},{1,5},{5... | collective-permute-start | bytes 3145736 | tf_op jit(solution)/shard_map/ppermute | solution.py:14
  394.5 6.0 %copy-start.1 = (f32[1024,512]{1,0:T(8,128)S(1)}, f32[1024,512]{1,0:T(8,128)}, u32[]{:S(2)}) copy-start(f32[1024,512]{1,0:T(8,128)} %param.2) | copy-start | bytes 6291460
  (33 other events, 66.2 us)
Sparse Core Ops, SparseCore 0:
  13.4 55.1 all-reduce.2
  168.4 24.6 all-gather.4
  276.7 24.6 all-gather.6
